TPU v7x, 32 devices: a whole 2x2x4 slice. The times are simulated.
32 devices in a mesh: rep: 8 (over y, x, core), shard: 4 (over z).
Axes of the slice: x: 2, y: 2, z: 4, core: 2. Of those that a mesh axis runs over, the one named last changes fastest.
Arguments:
- inputs: bfloat16 [8, 4, 1104, 1024], P('rep', 'shard'), may hold values from -6 to 6
- counts: int32 [8], P('rep'), may hold values from 1 to 4, as said below
- ln1_gain: bfloat16 [1024], P('shard'), may hold values from 0.5 to 1.5
- ln1_shift: bfloat16 [1024], P('shard'), may hold values from -4 to 4
- w_qkv: bfloat16 [1024, 3072], P('shard'), may hold values from -0.1875 to 0.1875
- qv_bias: bfloat16 [2048], P('shard'), may hold values from -4 to 4
- w_out: bfloat16 [1024, 1024], P('shard'), may hold values from -0.75 to 0.75
- out_bias: bfloat16 [1024], P('shard'), may hold values from -4 to 4
- ln2_gain: bfloat16 [1024], P('shard'), may hold values from 0.5 to 1.5
- ln2_shift: bfloat16 [1024], P('shard'), may hold values from -4 to 4
- w_up: bfloat16 [1024, 4096], P('shard'), may hold values from -0.1875 to 0.1875
- up_bias: bfloat16 [4096], P('shard'), may hold values from -4 to 4
- w_down: bfloat16 [4096, 1024], P('shard'), may hold values from -0.09375 to 0.09375
- down_bias: bfloat16 [1024], P('shard'), may hold values from -4 to 4
- cotangent: bfloat16 [8, 4, 1104, 1024], P('rep', 'shard'), may hold values from -6 to 6
Outputs:
- output: bfloat16 [8, 4, 1104, 1024], P('rep', 'shard')
- input_grad: float32 [8, 4, 1104, 1024], P('rep', 'shard')
- grad_ln1_gain: float32 [1024], P('shard')
- grad_ln1_shift: float32 [1024], P('shard')
- grad_w_qkv: float32 [1024, 3072], P('shard')
- grad_qv_bias: float32 [2048], P('shard')
- grad_w_out: float32 [1024, 1024], P('shard')
- grad_out_bias: float32 [1024], P('shard')
- grad_ln2_gain: float32 [1024], P('shard')
- grad_ln2_shift: float32 [1024], P('shard')
- grad_w_up: float32 [1024, 4096], P('shard')
- grad_up_bias: float32 [4096], P('shard')
- grad_w_down: float32 [4096, 1024], P('shard')
- grad_down_bias: float32 [1024], P('shard')
Inputs may be any that keep to these rules, and one draw needn't show every extreme that they name: A group's live sequences occupy its slots 0 to counts - 1; some group has exactly 4 and some exactly 1.
All inputs are finite; a program needn't handle non-finite values.
Results may differ from a plain program's by a relative error of at most 0.018.
Values may be sent and summed in bfloat16 or wider, within the bound.
No kernel may reach another device: no remote copies, remote signals or barrier semaphores. Data moves between devices by JAX's collectives and lax.ppermute only.
A program may use at most 256 MiB of HBM per device.

v0:
```python
import jax
import jax.numpy as jnp
from jax import lax
from jax.sharding import PartitionSpec as P

HEADS = 16
HDIM = 64
eps = 1e-06
head_block = 4


def layer_norm(values, gain, shift):
    centre = values - jnp.mean(values, -1, keepdims=True)
    spread = jnp.mean(centre * centre, -1, keepdims=True)
    return centre * lax.rsqrt(spread + eps) * gain + shift


def gelu_exact(values):
    return jax.nn.gelu(values, approximate=False)


def matmul(left, right):
    return jnp.dot(left, right, preferred_element_type=jnp.float32)


def left_trans(left, right):
    return lax.dot_general(
        left, right, (((0,), (0,)), ((), ())), preferred_element_type=jnp.float32
    )


def right_trans(left, right):
    return lax.dot_general(
        left, right, (((1,), (1,)), ((), ())), preferred_element_type=jnp.float32
    )


def body(
    inputs,
    counts,
    ln1_gain,
    ln1_shift,
    w_qkv,
    qv_bias,
    w_out,
    out_bias,
    ln2_gain,
    ln2_shift,
    w_up,
    up_bias,
    w_down,
    down_bias,
    cotangent,
):
    gathered = (
        lax.all_gather(ln1_gain, "shard", axis=0, tiled=True),
        lax.all_gather(ln1_shift, "shard", axis=0, tiled=True),
        lax.all_gather(w_qkv, "shard", axis=0, tiled=True),
        lax.all_gather(qv_bias, "shard", axis=0, tiled=True),
        lax.all_gather(w_out, "shard", axis=0, tiled=True),
        lax.all_gather(out_bias, "shard", axis=0, tiled=True),
        lax.all_gather(ln2_gain, "shard", axis=0, tiled=True),
        lax.all_gather(ln2_shift, "shard", axis=0, tiled=True),
        lax.all_gather(w_up, "shard", axis=0, tiled=True),
        lax.all_gather(up_bias, "shard", axis=0, tiled=True),
        lax.all_gather(w_down, "shard", axis=0, tiled=True),
        lax.all_gather(down_bias, "shard", axis=0, tiled=True),
    )
    (
        full_g1,
        full_s1,
        full_qkv,
        full_qvb,
        full_wout,
        full_bout,
        full_g2,
        full_s2,
        full_wup,
        full_bup,
        full_wdown,
        full_bdown,
    ) = gathered
    slots = inputs.shape[1]
    seq_len = inputs.shape[2]
    width = inputs.shape[3]
    n_rows = slots * seq_len
    groups = HEADS // head_block
    scale = HDIM ** (-0.5)
    first_slot = lax.axis_index("shard") * slots
    alive = (jnp.arange(slots, dtype=jnp.int32) + first_slot < counts[0]).astype(jnp.float32)
    alive_rows = jnp.broadcast_to(alive[:, None], (slots, seq_len)).reshape(n_rows, 1)
    tokens = inputs.reshape(n_rows, width).astype(jnp.float32)
    hidden_one, norm_one_back = jax.vjp(
        layer_norm, tokens, full_g1.astype(jnp.float32), full_s1.astype(jnp.float32)
    )
    hidden_one_b = hidden_one.astype(jnp.bfloat16)
    projected = matmul(hidden_one_b, full_qkv)
    bias_f = full_qvb.astype(jnp.float32)
    queries_b = (projected[:, :width] + bias_f[:width]).astype(jnp.bfloat16)
    keys_b = projected[:, width : 2 * width].astype(jnp.bfloat16)
    values_b = (projected[:, 2 * width :] + bias_f[width:]).astype(jnp.bfloat16)

    def arrange(values):
        return values.reshape(slots, seq_len, groups, head_block, HDIM).transpose(2, 0, 1, 3, 4)

    def restore(values):
        return values.transpose(1, 2, 0, 3, 4).reshape(n_rows, width)

    query_groups = arrange(queries_b)
    key_groups = arrange(keys_b)
    value_groups = arrange(values_b)

    def forward_group(operands):
        query_part, key_part, value_part = operands
        scores = (
            jnp.einsum("cqhd,ckhd->chqk", query_part, key_part, preferred_element_type=jnp.float32)
            * scale
        )
        largest = jnp.max(scores, -1, keepdims=True)
        exponent = jnp.exp(scores - largest)
        denominator = jnp.sum(exponent, -1, keepdims=True)
        probs_b = (exponent / denominator).astype(jnp.bfloat16)
        mixed = jnp.einsum(
            "chqk,ckhd->cqhd", probs_b, value_part, preferred_element_type=jnp.float32
        )
        return (mixed, (largest + jnp.log(denominator))[..., 0])

    mixed_groups, log_totals = lax.map(forward_group, (query_groups, key_groups, value_groups))
    attended_b = restore(mixed_groups).astype(jnp.bfloat16)
    middle = tokens + matmul(attended_b, full_wout) + full_bout.astype(jnp.float32)
    hidden_two, norm_two_back = jax.vjp(
        layer_norm, middle, full_g2.astype(jnp.float32), full_s2.astype(jnp.float32)
    )
    hidden_two_b = hidden_two.astype(jnp.bfloat16)
    pre_act = matmul(hidden_two_b, full_wup) + full_bup.astype(jnp.float32)
    activated, gelu_back = jax.vjp(gelu_exact, pre_act)
    activated_b = activated.astype(jnp.bfloat16)
    result = middle + matmul(activated_b, full_wdown) + full_bdown.astype(jnp.float32)
    output = (alive_rows * result).astype(jnp.bfloat16).reshape(inputs.shape)
    again = (
        lax.all_gather(ln1_gain, "shard", axis=0, tiled=True),
        lax.all_gather(ln1_shift, "shard", axis=0, tiled=True),
        lax.all_gather(w_qkv, "shard", axis=0, tiled=True),
        lax.all_gather(qv_bias, "shard", axis=0, tiled=True),
        lax.all_gather(w_out, "shard", axis=0, tiled=True),
        lax.all_gather(out_bias, "shard", axis=0, tiled=True),
        lax.all_gather(ln2_gain, "shard", axis=0, tiled=True),
        lax.all_gather(ln2_shift, "shard", axis=0, tiled=True),
        lax.all_gather(w_up, "shard", axis=0, tiled=True),
        lax.all_gather(up_bias, "shard", axis=0, tiled=True),
        lax.all_gather(w_down, "shard", axis=0, tiled=True),
        lax.all_gather(down_bias, "shard", axis=0, tiled=True),
    )
    back_qkv = again[2]
    back_wout = again[4]
    back_wup = again[8]
    back_wdown = again[10]
    d_out = alive_rows * cotangent.reshape(n_rows, width).astype(jnp.float32)
    d_out_b = d_out.astype(jnp.bfloat16)
    grad_wdown = left_trans(activated_b, d_out_b)
    grad_bdown = jnp.sum(d_out, 0)
    d_act = right_trans(d_out_b, back_wdown)
    d_pre_b = gelu_back(d_act)[0].astype(jnp.bfloat16)
    grad_wup = left_trans(hidden_two_b, d_pre_b)
    grad_bup = jnp.sum(d_pre_b.astype(jnp.float32), 0)
    d_hidden_two = right_trans(d_pre_b, back_wup)
    d_mid_norm, grad_g2, grad_s2 = norm_two_back(d_hidden_two)
    d_mid = d_out + d_mid_norm
    d_proj_b = d_mid.astype(jnp.bfloat16)
    grad_wout = left_trans(attended_b, d_proj_b)
    grad_bout = jnp.sum(d_proj_b.astype(jnp.float32), 0)
    d_att_b = right_trans(d_proj_b, back_wout).astype(jnp.bfloat16)
    d_att_groups = arrange(d_att_b)

    def backward_group(operands):
        query_part, key_part, value_part, log_total, grad_part = operands
        scores = (
            jnp.einsum("cqhd,ckhd->chqk", query_part, key_part, preferred_element_type=jnp.float32)
            * scale
        )
        attn_probs = jnp.exp(scores - log_total[..., None])
        probs_b = attn_probs.astype(jnp.bfloat16)
        d_probs = jnp.einsum(
            "cqhd,ckhd->chqk", grad_part, value_part, preferred_element_type=jnp.float32
        )
        row_inner = jnp.sum(d_probs * attn_probs, -1, keepdims=True)
        d_scores_b = (attn_probs * (d_probs - row_inner)).astype(jnp.bfloat16)
        d_query = (
            jnp.einsum("chqk,ckhd->cqhd", d_scores_b, key_part, preferred_element_type=jnp.float32)
            * scale
        )
        d_key = (
            jnp.einsum(
                "chqk,cqhd->ckhd", d_scores_b, query_part, preferred_element_type=jnp.float32
            )
            * scale
        )
        d_value = jnp.einsum(
            "chqk,cqhd->ckhd", probs_b, grad_part, preferred_element_type=jnp.float32
        )
        return (d_query, d_key, d_value)

    d_query_groups, d_key_groups, d_value_groups = lax.map(
        backward_group, (query_groups, key_groups, value_groups, log_totals, d_att_groups)
    )
    d_qkv_b = jnp.concatenate(
        [restore(d_query_groups), restore(d_key_groups), restore(d_value_groups)], 1
    ).astype(jnp.bfloat16)
    grad_qkv = left_trans(hidden_one_b, d_qkv_b)
    column_sums = jnp.sum(d_qkv_b.astype(jnp.float32), 0)
    grad_qvb = jnp.concatenate([column_sums[:width], column_sums[2 * width :]])
    d_hidden_one = right_trans(d_qkv_b, back_qkv)
    d_in_norm, grad_g1, grad_s1 = norm_one_back(d_hidden_one)
    input_grad = (d_mid + d_in_norm).reshape(inputs.shape)
    owned = (
        lax.psum_scatter(
            grad_g1.astype(jnp.bfloat16), "shard", scatter_dimension=0, tiled=True
        ).astype(jnp.float32),
        lax.psum_scatter(
            grad_s1.astype(jnp.bfloat16), "shard", scatter_dimension=0, tiled=True
        ).astype(jnp.float32),
        lax.psum_scatter(
            grad_qkv.astype(jnp.bfloat16), "shard", scatter_dimension=0, tiled=True
        ).astype(jnp.float32),
        lax.psum_scatter(
            grad_qvb.astype(jnp.bfloat16), "shard", scatter_dimension=0, tiled=True
        ).astype(jnp.float32),
        lax.psum_scatter(
            grad_wout.astype(jnp.bfloat16), "shard", scatter_dimension=0, tiled=True
        ).astype(jnp.float32),
        lax.psum_scatter(
            grad_bout.astype(jnp.bfloat16), "shard", scatter_dimension=0, tiled=True
        ).astype(jnp.float32),
        lax.psum_scatter(
            grad_g2.astype(jnp.bfloat16), "shard", scatter_dimension=0, tiled=True
        ).astype(jnp.float32),
        lax.psum_scatter(
            grad_s2.astype(jnp.bfloat16), "shard", scatter_dimension=0, tiled=True
        ).astype(jnp.float32),
        lax.psum_scatter(
            grad_wup.astype(jnp.bfloat16), "shard", scatter_dimension=0, tiled=True
        ).astype(jnp.float32),
        lax.psum_scatter(
            grad_bup.astype(jnp.bfloat16), "shard", scatter_dimension=0, tiled=True
        ).astype(jnp.float32),
        lax.psum_scatter(
            grad_wdown.astype(jnp.bfloat16), "shard", scatter_dimension=0, tiled=True
        ).astype(jnp.float32),
        lax.psum_scatter(
            grad_bdown.astype(jnp.bfloat16), "shard", scatter_dimension=0, tiled=True
        ).astype(jnp.float32),
    )
    o_g1, o_s1, o_qkv, o_qvb, o_wout, o_bout, o_g2, o_s2, o_wup, o_bup, o_wdown, o_bdown = owned
    summed = (
        lax.psum(o_g1.astype(jnp.bfloat16), "rep").astype(jnp.float32),
        lax.psum(o_s1.astype(jnp.bfloat16), "rep").astype(jnp.float32),
        lax.psum(o_qkv.astype(jnp.bfloat16), "rep").astype(jnp.float32),
        lax.psum(o_qvb.astype(jnp.bfloat16), "rep").astype(jnp.float32),
        lax.psum(o_wout.astype(jnp.bfloat16), "rep").astype(jnp.float32),
        lax.psum(o_bout.astype(jnp.bfloat16), "rep").astype(jnp.float32),
        lax.psum(o_g2.astype(jnp.bfloat16), "rep").astype(jnp.float32),
        lax.psum(o_s2.astype(jnp.bfloat16), "rep").astype(jnp.float32),
        lax.psum(o_wup.astype(jnp.bfloat16), "rep").astype(jnp.float32),
        lax.psum(o_bup.astype(jnp.bfloat16), "rep").astype(jnp.float32),
        lax.psum(o_wdown.astype(jnp.bfloat16), "rep").astype(jnp.float32),
        lax.psum(o_bdown.astype(jnp.bfloat16), "rep").astype(jnp.float32),
    )
    return (
        output,
        input_grad,
        summed[0],
        summed[1],
        summed[2],
        summed[3],
        summed[4],
        summed[5],
        summed[6],
        summed[7],
        summed[8],
        summed[9],
        summed[10],
        summed[11],
    )


def solution(mesh):
    placed = (
        P("rep", "shard", None, None),
        P("rep"),
        P("shard"),
        P("shard"),
        P("shard", None),
        P("shard"),
        P("shard", None),
        P("shard"),
        P("shard"),
        P("shard"),
        P("shard", None),
        P("shard"),
        P("shard", None),
        P("shard"),
        P("rep", "shard", None, None),
    )
    return jax.shard_map(
        body,
        mesh=mesh,
        in_specs=placed,
        out_specs=(
            P("rep", "shard", None, None),
            P("rep", "shard", None, None),
            P("shard"),
            P("shard"),
            P("shard", None),
            P("shard"),
            P("shard", None),
            P("shard"),
            P("shard"),
            P("shard"),
            P("shard", None),
            P("shard"),
            P("shard", None),
            P("shard"),
        ),
        check_vma=False,
    )
```

profile of v0, /device:TPU:0, one launch (start us, length us, event | category | flops | bytes accessed | tf_op | source)
XLA Modules:
  0.0 1330.5 jit_solution(4466956774392505986)
XLA Ops:
  10.9 12.6 all-gather.5
  32.4 12.4 all-gather.3
  53.3 14.0 %all-gather = bf16[4,1,256]{2,1,0:T(2,128)(2,1)S(1)} all-gather(bf16[1,1,256]{2,1,0:T(2,128)(2,1)S(1)} %reshape.260), channel_id=1, replica_groups=mesh['rep'=8,'shard'=4] {'shard'}, dimensions={0}, use_global_device_ids=true | all-gather | bytes 2560 | tf_op jit(solution)/shard_map/all_gather | solution.py:56
  67.3 12.1 all-gather.2
  79.4 16.0 %all_gather.49 = bf16[4096]{0:T(1024)(128)(2,1)S(1)} all-gather(bf16[1024]{0:T(1024)(128)(2,1)S(1)} %copy-done.47), channel_id=1, replica_groups=mesh['rep'=8,'shard'=4] {'shard'}, dimensions={0}, use_global_device_ids=true | all-gather | bytes 10240 | tf_op jit(solution)/shard_map/all_gather | solution.py:65
  97.8 30.4 %all-gather.12.cloned.1.call-done = bf16[1024,3072]{1,0:T(8,128)(2,1)} async-done(((bf16[256,3072]{1,0:T(8,128)(2,1)}), bf16[1024,3072]{1,0:T(8,128)(2,1)}) %all-gather.12.cloned.1.call-update) | async-done | bytes 6291472 | tf_op jit(solution)/shard_map/all_gather | solution.py:58
  156.2 131.5 %while.26 = (s32[]{:T(128)}, bf16[4,1,1104,4,64]{2,4,3,1,0:T(8,128)(2,1)}, f32[4,1,4,1104]{3,2,1,0:T(4,128)}, bf16[4,1,1104,4,64]{2,4,3,1,0:T(8,128)(2,1)}, bf16...) while((s32[]{:T(128)}, bf16[4,1,1104,4,64]{2,4,3,1,0:T(8,128)(2,1)}, ...), condition=%wide.region_5.6_spmd, body=%wide.region_2.5_spmd.sunk | while | flops 1282190080 | bytes 62444376 | solution.py:128
  156.3 10.7 fusion.129
  176.6 12.7 fusion.131
  189.9 10.7 fusion.129
  200.7 9.7 fusion.130
  210.3 11.5 fusion.131
  222.5 10.7 fusion.129
  242.9 11.5 fusion.131
  255.0 10.7 fusion.129
  275.4 11.5 fusion.131
  297.9 26.0 %all-gather.16.cloned.1.call-done = bf16[1024,4096]{1,0:T(8,128)(2,1)} async-done(((bf16[256,4096]{1,0:T(8,128)(2,1)}), bf16[1024,4096]{1,0:T(8,128)(2,1)}) %all-gather.16.cloned.1.call-update) | async-done | bytes 8388624 | tf_op jit(solution)/shard_map/all_gather | solution.py:64
  323.9 54.4 %multiply_convert_fusion.1 = (bf16[1104,4096]{1,0:T(8,128)(2,1)}, f32[1104,4096]{1,0:T(8,128)}, f32[1104,4096]{1,0:T(8,128)}) fusion(f32[4096]{0:T(1024)S(1)} %copy-done.39, bf16[1024,4096]{1,0:T(8,128)(2,1)} %all-gather.16.cloned.1.call-done, f32[1104,1024]{1,0:T(8,128)} %copy-done.8, f32[1024]{0:T(1024)S(1)} %bitcast.254, f32[1024]{0:T(1024)S(1)} %bitcast.248, ...), kind=kOutput, calls=%fused_computation.56 | convolution fusion | flops 9565126656 | bytes 58163840 | tf_op jit(solution)/shard_map/dot_general | solution.py:23
  378.3 94.9 %all-gather.18.cloned.1.call-done = bf16[4096,1024]{1,0:T(8,128)(2,1)} async-done(((bf16[1024,1024]{1,0:T(8,128)(2,1)}), bf16[4096,1024]{1,0:T(8,128)(2,1)}) %all-gather.18.cloned.1.call-update) | async-done | bytes 8388624 | tf_op jit(solution)/shard_map/all_gather | solution.py:66
  473.2 25.4 %fusion.92 = (bf16[4096]{0:T(1024)(128)(2,1)}, bf16[1104,4096]{1,0:T(8,128)(2,1)}) fusion(f32[1104,4096]{1,0:T(8,128)} %get-tuple-element.193, f32[1104,4096]{1,0:T(8,128)} %get-tuple-element.206, bf16[4096,1024]{1,0:T(8,128)(2,1)} %all-gather.18.cloned.1.call-done, bf16[1,1,1104,1024]{3,2,1,0:T(8,128)(2,1)S(1)} %copy-done.6, f32[]{:T(128)} %bitcast.22), kind=kOutput, calls=%fused_computation.137 | convolution fusion | flops 9332240384 | bytes 55877636 | tf_op jit(solution)/shard_map/dot_general | solution.py:33
  498.6 18.1 %multiply_reduce_fusion.1 = (bf16[1024]{0:T(1024)(128)(2,1)}, f32[1104]{0:T(1024)S(1)}, bf16[1024]{0:T(1024)(128)(2,1)}, f32[1104,1024]{1,0:T(8,128)S(1)}) fusion(f32[1104,1024]{1,0:T(8,128)} %copy-done.8, f32[1104]{0:T(1024)S(1)} %fusion.76, f32[1104]{0:T(1024)S(1)} %broadcast_multiply_fusion, f32[1024]{0:T(1024)S(1)} %bitcast.249, ...), kind=kOutput, calls=%fused_computation.102 | convolution fusion | flops 9270064128 | bytes 26497984 | tf_op jit(solution)/shard_map/dot_general | solution.py:33
  538.8 243.8 %while.27 = (s32[]{:T(128)}, bf16[4,1,1104,4,64]{2,4,3,1,0:T(8,128)(2,1)}, bf16[4,1,1104,4,64]{2,4,3,1,0:T(8,128)(2,1)}, bf16[4,1,1104,4,64]{2,4,3,1,0:T(8,128)(...) while((s32[]{:T(128)}, ...), condition=%wide.region_12.13_spmd, body=%wide.region_10.12_spmd.sunk | while | flops 3159731968 | bytes 219023680 | solution.py:203
  539.5 11.1 fusion.140
  550.6 10.1 fusion.143
  560.7 17.6 %multiply_reduce_fusion.5 = (f32[4,1104]{1,0:T(4,128)S(1)}, f32[4,1104,1104]{1,2,0:T(8,128)}) fusion(f32[4,1104,1104]{1,2,0:T(8,128)} %fusion.140, bf16[4,1,1104,4,64]{2,4,3,1,0:T(8,128)(2,1)} %get-tuple-element.360, s32[]{:T(128)S(6)} %copy.89, bf16[4,1,1104,4,64]{2,4,3,1,0:T(8,128)(2,1)S(1)} %copy-done.5), kind=kOutput, calls=%fused_computation.20.clone.1 | convolution fusion | flops 633779904 | bytes 41048320 | tf_op jit(solution)/shard_map/while/body/eval_jaxpr/cqhd,ckhd->chqk/dot_general | solution.py:183
  578.4 13.5 %multiply_convert_fusion.3 = bf16[4,1104,1104]{1,2,0:T(8,128)(2,1)S(1)} fusion(f32[4,1104,1104]{1,2,0:T(8,128)} %fusion.140, f32[4,1104,1104]{1,2,0:T(8,128)} %get-tuple-element.309, f32[4,1104]{1,0:T(4,128)S(1)} %get-tuple-element.310), kind=kLoop, calls=%fused_computation.19.clone.1 | loop fusion | flops 14625792 | bytes 48770304 | tf_op jit(solution)/shard_map/while/body/eval_jaxpr/convert_element_type | solution.py:187
  600.6 11.0 fusion.140
  611.7 10.0 fusion.143
  621.6 17.5 %multiply_reduce_fusion.5 = (f32[4,1104]{1,0:T(4,128)S(1)}, f32[4,1104,1104]{1,2,0:T(8,128)}) fusion(f32[4,1104,1104]{1,2,0:T(8,128)} %fusion.140, bf16[4,1,1104,4,64]{2,4,3,1,0:T(8,128)(2,1)} %get-tuple-element.360, s32[]{:T(128)S(6)} %copy.89, bf16[4,1,1104,4,64]{2,4,3,1,0:T(8,128)(2,1)S(1)} %copy-done.5), kind=kOutput, calls=%fused_computation.20.clone.1 | convolution fusion | flops 633779904 | bytes 41048320 | tf_op jit(solution)/shard_map/while/body/eval_jaxpr/cqhd,ckhd->chqk/dot_general | solution.py:183
  639.2 13.5 %multiply_convert_fusion.3 = bf16[4,1104,1104]{1,2,0:T(8,128)(2,1)S(1)} fusion(f32[4,1104,1104]{1,2,0:T(8,128)} %fusion.140, f32[4,1104,1104]{1,2,0:T(8,128)} %get-tuple-element.309, f32[4,1104]{1,0:T(4,128)S(1)} %get-tuple-element.310), kind=kLoop, calls=%fused_computation.19.clone.1 | loop fusion | flops 14625792 | bytes 48770304 | tf_op jit(solution)/shard_map/while/body/eval_jaxpr/convert_element_type | solution.py:187
  661.5 11.0 fusion.140
  672.5 10.0 fusion.143
  682.5 17.5 %multiply_reduce_fusion.5 = (f32[4,1104]{1,0:T(4,128)S(1)}, f32[4,1104,1104]{1,2,0:T(8,128)}) fusion(f32[4,1104,1104]{1,2,0:T(8,128)} %fusion.140, bf16[4,1,1104,4,64]{2,4,3,1,0:T(8,128)(2,1)} %get-tuple-element.360, s32[]{:T(128)S(6)} %copy.89, bf16[4,1,1104,4,64]{2,4,3,1,0:T(8,128)(2,1)S(1)} %copy-done.5), kind=kOutput, calls=%fused_computation.20.clone.1 | convolution fusion | flops 633779904 | bytes 41048320 | tf_op jit(solution)/shard_map/while/body/eval_jaxpr/cqhd,ckhd->chqk/dot_general | solution.py:183
  700.0 13.5 %multiply_convert_fusion.3 = bf16[4,1104,1104]{1,2,0:T(8,128)(2,1)S(1)} fusion(f32[4,1104,1104]{1,2,0:T(8,128)} %fusion.140, f32[4,1104,1104]{1,2,0:T(8,128)} %get-tuple-element.309, f32[4,1104]{1,0:T(4,128)S(1)} %get-tuple-element.310), kind=kLoop, calls=%fused_computation.19.clone.1 | loop fusion | flops 14625792 | bytes 48770304 | tf_op jit(solution)/shard_map/while/body/eval_jaxpr/convert_element_type | solution.py:187
  722.3 11.0 fusion.140
  733.3 10.0 fusion.143
  743.3 17.5 %multiply_reduce_fusion.5 = (f32[4,1104]{1,0:T(4,128)S(1)}, f32[4,1104,1104]{1,2,0:T(8,128)}) fusion(f32[4,1104,1104]{1,2,0:T(8,128)} %fusion.140, bf16[4,1,1104,4,64]{2,4,3,1,0:T(8,128)(2,1)} %get-tuple-element.360, s32[]{:T(128)S(6)} %copy.89, bf16[4,1,1104,4,64]{2,4,3,1,0:T(8,128)(2,1)S(1)} %copy-done.5), kind=kOutput, calls=%fused_computation.20.clone.1 | convolution fusion | flops 633779904 | bytes 41048320 | tf_op jit(solution)/shard_map/while/body/eval_jaxpr/cqhd,ckhd->chqk/dot_general | solution.py:183
  760.9 13.5 %multiply_convert_fusion.3 = bf16[4,1104,1104]{1,2,0:T(8,128)(2,1)S(1)} fusion(f32[4,1104,1104]{1,2,0:T(8,128)} %fusion.140, f32[4,1104,1104]{1,2,0:T(8,128)} %get-tuple-element.309, f32[4,1104]{1,0:T(4,128)S(1)} %get-tuple-element.310), kind=kLoop, calls=%fused_computation.19.clone.1 | loop fusion | flops 14625792 | bytes 48770304 | tf_op jit(solution)/shard_map/while/body/eval_jaxpr/convert_element_type | solution.py:187
  782.6 15.3 %convolution_convert_fusion.2 = bf16[1024,3072]{1,0:T(8,128)(2,1)} fusion(bf16[1,1,1104,1024]{3,2,1,0:T(8,128)(2,1)} %param.19, f32[1024]{0:T(1024)S(1)} %bitcast.257, f32[1024]{0:T(1024)S(1)} %bitcast.244, f32[1104]{0:T(1024)S(1)} %copy-done.24, f32[1104]{0:T(1024)S(1)} %copy-done.22, bf16[1104,1024]{0,1:T(8,128)(2,1)} %bitcast.232, ...), kind=kOutput, calls=%fused_computation.75 | convolution fusion | flops 6976045056 | bytes 15352448 | tf_op jit(solution)/shard_map/dot_general | solution.py:27
  798.6 18.7 %convolution_convert_fusion.1 = bf16[1024,4096]{1,0:T(8,128)(2,1)} fusion(bf16[1104,4096]{1,0:T(8,128)(2,1)} %get-tuple-element.210, f32[1104,1024]{1,0:T(8,128)} %copy-done.8, f32[1024]{0:T(1024)S(1)} %bitcast.255, f32[1024]{0:T(1024)S(1)} %bitcast.251, f32[1104]{0:T(1024)S(1)} %copy-done.36, f32[1104]{0:T(1024)S(1)} %copy-done.26), kind=kOutput, calls=%fused_computation.71 | convolution fusion | flops 9270870016 | bytes 21971584 | tf_op jit(solution)/shard_map/dot_general | solution.py:27
  818.9 17.4 %convolution_convert_fusion = bf16[4096,1024]{1,0:T(8,128)(2,1)} fusion(bf16[1104,4096]{1,0:T(8,128)(2,1)} %get-tuple-element.192, bf16[1,1,1104,1024]{3,2,1,0:T(8,128)(2,1)S(1)} %copy-done.7, f32[]{:T(128)} %bitcast.22), kind=kOutput, calls=%fused_computation.70 | convolution fusion | flops 9268609024 | bytes 19693572 | tf_op jit(solution)/shard_map/dot_general | solution.py:27
  854.6 12.6 fusion.83
  872.0 22.2 %all-reduce.10 = (bf16[1024]{0:T(1024)(128)(2,1)S(1)}, bf16[1024]{0:T(1024)(128)(2,1)S(1)}, bf16[2048]{0:T(1024)(128)(2,1)S(1)}, bf16[1024]{0:T(1024)(128)(2,1)S...) all-reduce(bf16[1024]{0:T(1024)(128)(2,1)S(1)} %get-tuple-element.1, ...), channel_id=2, replica_groups=mesh['rep'=8,'shard'=4] {'shard'}, use_global_device_ids=true, to_apply=%region_16.17.clone | all-reduce | flops 12288 | bytes 49152
  894.8 12.5 all-reduce.8
  911.8 143.8 %reduce-scatter.9.cloned.1.call-done = bf16[256,4096]{1,0:T(8,128)(2,1)} async-done(((bf16[1024,4096]{1,0:T(8,128)(2,1)}), bf16[256,4096]{1,0:T(8,128)(2,1)}) %reduce-scatter.9.cloned.1.call-update) | async-done | bytes 2097168 | tf_op jit(solution)/shard_map/reduce_scatter | solution.py:240
  1055.6 147.7 %reduce-scatter.11.cloned.1.call-done = bf16[1024,1024]{1,0:T(8,128)(2,1)} async-done(((bf16[4096,1024]{1,0:T(8,128)(2,1)}), bf16[1024,1024]{1,0:T(8,128)(2,1)}) %reduce-scatter.11.cloned.1.call-update) | async-done | bytes 2097168 | tf_op jit(solution)/shard_map/reduce_scatter | solution.py:246
  1210.1 17.3 %fusion.72 = bf16[1,1,1104,1024]{3,2,1,0:T(8,128)(2,1)} fusion(f32[1104,1024]{1,0:T(8,128)} %copy-done.8, bf16[1104,4096]{1,0:T(8,128)(2,1)} %get-tuple-element.192, bf16[4096,1024]{1,0:T(8,128)(2,1)} %all-gather.18.cloned.1.call-done, f32[1024]{0:T(1024)S(1)} %bitcast.258, f32[]{:T(128)} %bitcast.22), kind=kOutput, calls=%fused_computation.111 | convolution fusion | flops 9265545216 | bytes 24219652 | tf_op jit(solution)/shard_map/dot_general | solution.py:23
  1227.4 85.5 %all-reduce.13.cloned.1.call-done = (bf16[256,3072]{1,0:T(8,128)(2,1)}, bf16[256,1024]{1,0:T(8,128)(2,1)}, bf16[256,4096]{1,0:T(8,128)(2,1)}, bf16[1024,1024]{1,0:T(8,128)(2,1)}) async-done(((bf16[256,3072]{1,0:T(8,128)(2,1)}, bf16[256,1024]{1,0:T(8,128)(2,1)}, bf16[256,4096]{1,0:T(8,128)(2,1)}, bf16[1024,1024]{1,0:T(8,128)(2,1)}), (bf16[256,3072]{1,0:T(8,128)(2,1)}, bf16[256,1024]{1,0:T(8,128)(2,1)}, ...) | async-done | bytes 6291472 | tf_op jit(solution)/shard_map/psum | solution.py:257
  (271 shorter events, 194.6 us)
Async XLA Ops:
  7.2 72.2 %copy-start.47 = (bf16[1024]{0:T(1024)(128)(2,1)S(1)}, bf16[1024]{0:T(1024)(128)(2,1)}, u32[]{:S(2)}) copy-start(bf16[1024]{0:T(1024)(128)(2,1)} %param.30) | copy-start | bytes 6148
  7.3 88.8 %copy-start.3 = (bf16[1,1,1104,1024]{3,2,1,0:T(8,128)(2,1)S(1)}, bf16[1,1,1104,1024]{3,2,1,0:T(8,128)(2,1)}, u32[]{:S(2)}) copy-start(bf16[1,1,1104,1024]{3,2,1,0:T(8,128)(2,1)} %param.19) | copy-start | bytes 6782980
  7.3 120.9 %all-gather.12.cloned.1.call-start = ((), (), s32[]{:S(2)}) async-start(), calls=%async_computation.4 | async-start | bytes 7864320 | tf_op jit(solution)/shard_map/all_gather | solution.py:58
  8.0 279.7 %all-gather.14.cloned.1.call-start = ((), (), s32[]{:S(2)}) async-start(), calls=%async_computation.5 | async-start | bytes 2621440 | tf_op jit(solution)/shard_map/all_gather | solution.py:60
  8.7 315.1 %all-gather.16.cloned.1.call-start = ((), (), s32[]{:S(2)}) async-start(), calls=%async_computation.6 | async-start | bytes 10485760 | tf_op jit(solution)/shard_map/all_gather | solution.py:64
  9.5 463.7 %all-gather.18.cloned.1.call-start = ((), (), s32[]{:S(2)}) async-start(), calls=%async_computation.7 | async-start | bytes 10485760 | tf_op jit(solution)/shard_map/all_gather | solution.py:66
  10.1 901.8 %reduce-scatter.7.cloned.1.call-start = ((), (), s32[]{:S(2)}) async-start(), calls=%async_computation.9 | async-start | bytes 2621440 | tf_op jit(solution)/shard_map/reduce_scatter | solution.py:228
  53.3 84.6 %copy-start.44 = (f32[4,1,256]{2,1,0:T(1,128)}, f32[4,1,256]{2,1,0:T(1,128)S(1)}, u32[]{:S(2)}) copy-start(f32[4,1,256]{2,1,0:T(1,128)S(1)} %convert_element_type.230) | copy-start | bytes 12292
  67.3 70.5 %copy-start.33 = (f32[4,1,256]{2,1,0:T(1,128)}, f32[4,1,256]{2,1,0:T(1,128)S(1)}, u32[]{:S(2)}) copy-start(f32[4,1,256]{2,1,0:T(1,128)S(1)} %convert_element_type.229) | copy-start | bytes 12292
  96.4 41.4 %copy-start.21 = (f32[1104]{0:T(1024)}, f32[1104]{0:T(1024)S(1)}, u32[]{:S(2)}) copy-start(f32[1104]{0:T(1024)S(1)} %broadcast_multiply_fusion.1) | copy-start | bytes 13252
  97.8 40.1 %copy-start.23 = (f32[1104]{0:T(1024)}, f32[1104]{0:T(1024)S(1)}, u32[]{:S(2)}) copy-start(f32[1104]{0:T(1024)S(1)} %fusion.75) | copy-start | bytes 13252
  156.2 131.5 %copy-start.46 = (f32[4,1,256]{2,1,0:T(1,128)S(1)}, f32[4,1,256]{2,1,0:T(1,128)}, u32[]{:S(2)}) copy-start(f32[4,1,256]{2,1,0:T(1,128)} %convert_element_type.232) | copy-start | bytes 12292
  287.7 6.9 copy-start
  294.6 29.3 %copy-start.37 = (f32[4,1,256]{2,1,0:T(1,128)S(1)}, f32[4,1,256]{2,1,0:T(1,128)}, u32[]{:S(2)}) copy-start(f32[4,1,256]{2,1,0:T(1,128)} %convert_element_type.233) | copy-start | bytes 12292
  294.6 29.3 %copy-start.39 = (f32[4096]{0:T(1024)S(1)}, f32[4096]{0:T(1024)}, u32[]{:S(2)}) copy-start(f32[4096]{0:T(1024)} %convert_element_type.198) | copy-start | bytes 49156
  294.6 29.3 %copy-start.42 = (f32[4,1,256]{2,1,0:T(1,128)S(1)}, f32[4,1,256]{2,1,0:T(1,128)}, u32[]{:S(2)}) copy-start(f32[4,1,256]{2,1,0:T(1,128)} %convert_element_type.234) | copy-start | bytes 12292
  294.6 222.1 %copy-start.25 = (f32[1104]{0:T(1024)}, f32[1104]{0:T(1024)S(1)}, u32[]{:S(2)}) copy-start(f32[1104]{0:T(1024)S(1)} %broadcast_multiply_fusion) | copy-start | bytes 13252
  297.9 218.8 %copy-start.35 = (f32[1104]{0:T(1024)}, f32[1104]{0:T(1024)S(1)}, u32[]{:S(2)}) copy-start(f32[1104]{0:T(1024)S(1)} %fusion.76) | copy-start | bytes 13252
  323.9 149.3 %copy-start.6 = (bf16[1,1,1104,1024]{3,2,1,0:T(8,128)(2,1)S(1)}, bf16[1,1,1104,1024]{3,2,1,0:T(8,128)(2,1)}, u32[]{:S(2)}) copy-start(bf16[1,1,1104,1024]{3,2,1,0:T(8,128)(2,1)} %param.33) | copy-start | bytes 6782980
  498.6 18.1 %copy-start.30 = (f32[1104]{0:T(1024)S(1)}, f32[1104]{0:T(1024)}, u32[]{:S(2)}) copy-start(f32[1104]{0:T(1024)} %copy-done.29) | copy-start | bytes 13252
  498.6 18.2 %copy-start.9 = (f32[1104,1024]{1,0:T(8,128)S(1)}, f32[1104,1024]{1,0:T(8,128)}, u32[]{:S(2)}) copy-start(f32[1104,1024]{1,0:T(8,128)} %copy-done.8) | copy-start | bytes 13565956
  526.0 385.8 %reduce-scatter.5.cloned.1.call-start = ((), (), s32[]{:S(2)}) async-start(), calls=%async_computation.8 | async-start | bytes 7864320 | tf_op jit(solution)/shard_map/reduce_scatter | solution.py:222
  538.8 243.8 %copy-start.22 = (f32[1104]{0:T(1024)S(1)}, f32[1104]{0:T(1024)}, u32[]{:S(2)}) copy-start(f32[1104]{0:T(1024)} %copy-done.21) | copy-start | bytes 13252
  538.8 243.8 %copy-start.24 = (f32[1104]{0:T(1024)S(1)}, f32[1104]{0:T(1024)}, u32[]{:S(2)}) copy-start(f32[1104]{0:T(1024)} %copy-done.23) | copy-start | bytes 13252
  538.8 243.8 %copy-start.34 = (f32[4,1,256]{2,1,0:T(1,128)S(1)}, f32[4,1,256]{2,1,0:T(1,128)}, u32[]{:S(2)}) copy-start(f32[4,1,256]{2,1,0:T(1,128)} %copy-done.33) | copy-start | bytes 12292
  538.8 243.8 %copy-start.45 = (f32[4,1,256]{2,1,0:T(1,128)S(1)}, f32[4,1,256]{2,1,0:T(1,128)}, u32[]{:S(2)}) copy-start(f32[4,1,256]{2,1,0:T(1,128)} %copy-done.44) | copy-start | bytes 12292
  539.5 11.1 copy-start.5
  539.5 11.1 copy-start.11
  560.7 17.6 %copy-start.12 = (bf16[4,1,1104,4,64]{2,4,3,1,0:T(8,128)(2,1)}, bf16[4,1,1104,4,64]{2,4,3,1,0:T(8,128)(2,1)S(1)}, u32[]{:S(2)}) copy-start(bf16[4,1,1104,4,64]{2,4,3,1,0:T(8,128)(2,1)S(1)} %fusion.143) | copy-start | bytes 6782980 | tf_op jit(solution)/shard_map/while
  578.3 13.6 %copy-start.13 = (bf16[4,1,1104,4,64]{2,4,3,1,0:T(8,128)(2,1)S(1)}, bf16[4,1,1104,4,64]{2,4,3,1,0:T(8,128)(2,1)}, u32[]{:S(2)}) copy-start(bf16[4,1,1104,4,64]{2,4,3,1,0:T(8,128)(2,1)} %get-tuple-element.344) | copy-start | bytes 6782980 | tf_op jit(solution)/shard_map/while
  600.6 11.0 copy-start.5
  600.6 11.0 copy-start.11
  621.6 17.6 %copy-start.12 = (bf16[4,1,1104,4,64]{2,4,3,1,0:T(8,128)(2,1)}, bf16[4,1,1104,4,64]{2,4,3,1,0:T(8,128)(2,1)S(1)}, u32[]{:S(2)}) copy-start(bf16[4,1,1104,4,64]{2,4,3,1,0:T(8,128)(2,1)S(1)} %fusion.143) | copy-start | bytes 6782980 | tf_op jit(solution)/shard_map/while
  639.2 13.6 %copy-start.13 = (bf16[4,1,1104,4,64]{2,4,3,1,0:T(8,128)(2,1)S(1)}, bf16[4,1,1104,4,64]{2,4,3,1,0:T(8,128)(2,1)}, u32[]{:S(2)}) copy-start(bf16[4,1,1104,4,64]{2,4,3,1,0:T(8,128)(2,1)} %get-tuple-element.344) | copy-start | bytes 6782980 | tf_op jit(solution)/shard_map/while
  661.5 11.0 copy-start.5
  661.5 11.0 copy-start.11
  682.5 17.6 %copy-start.12 = (bf16[4,1,1104,4,64]{2,4,3,1,0:T(8,128)(2,1)}, bf16[4,1,1104,4,64]{2,4,3,1,0:T(8,128)(2,1)S(1)}, u32[]{:S(2)}) copy-start(bf16[4,1,1104,4,64]{2,4,3,1,0:T(8,128)(2,1)S(1)} %fusion.143) | copy-start | bytes 6782980 | tf_op jit(solution)/shard_map/while
  700.0 13.6 %copy-start.13 = (bf16[4,1,1104,4,64]{2,4,3,1,0:T(8,128)(2,1)S(1)}, bf16[4,1,1104,4,64]{2,4,3,1,0:T(8,128)(2,1)}, u32[]{:S(2)}) copy-start(bf16[4,1,1104,4,64]{2,4,3,1,0:T(8,128)(2,1)} %get-tuple-element.344) | copy-start | bytes 6782980 | tf_op jit(solution)/shard_map/while
  722.3 11.0 copy-start.5
  722.3 11.0 copy-start.11
  743.3 17.6 %copy-start.12 = (bf16[4,1,1104,4,64]{2,4,3,1,0:T(8,128)(2,1)}, bf16[4,1,1104,4,64]{2,4,3,1,0:T(8,128)(2,1)S(1)}, u32[]{:S(2)}) copy-start(bf16[4,1,1104,4,64]{2,4,3,1,0:T(8,128)(2,1)S(1)} %fusion.143) | copy-start | bytes 6782980 | tf_op jit(solution)/shard_map/while
  760.9 13.6 %copy-start.13 = (bf16[4,1,1104,4,64]{2,4,3,1,0:T(8,128)(2,1)S(1)}, bf16[4,1,1104,4,64]{2,4,3,1,0:T(8,128)(2,1)}, u32[]{:S(2)}) copy-start(bf16[4,1,1104,4,64]{2,4,3,1,0:T(8,128)(2,1)} %get-tuple-element.344) | copy-start | bytes 6782980 | tf_op jit(solution)/shard_map/while
  797.9 257.7 %reduce-scatter.9.cloned.1.call-start = ((), (), s32[]{:S(2)}) async-start(), calls=%async_computation.10 | async-start | bytes 10485760 | tf_op jit(solution)/shard_map/reduce_scatter | solution.py:240
  817.3 386.0 %reduce-scatter.11.cloned.1.call-start = ((), (), s32[]{:S(2)}) async-start(), calls=%async_computation.11 | async-start | bytes 10485760 | tf_op jit(solution)/shard_map/reduce_scatter | solution.py:246
  836.3 476.6 %all-reduce.13.cloned.1.call-start = ((), (), s32[]{:S(2)}) async-start(), calls=%async_computation.12 | async-start | bytes 12582912 | tf_op jit(solution)/shard_map/psum | solution.py:257
  847.6 7.0 copy-start.4
  854.6 12.7 copy-start.28
  872.0 331.4 %copy-start.32 = (f32[1104]{0:T(1024)S(1)}, f32[1104]{0:T(1024)}, u32[]{:S(2)}) copy-start(f32[1104]{0:T(1024)} %copy-done.31) | copy-start | bytes 13252
  (40 other events, 113.0 us)
Sparse Core Ops, SparseCore 0:
  9.7 118.4 all-gather.11
  129.7 44.1 all-gather.13
  175.5 148.3 all-gather.15
  325.3 147.8 all-gather.17
  526.1 42.0 reduce-scatter.6
  798.1 110.0 reduce-scatter.4
  910.7 144.9 reduce-scatter.8
  1058.1 145.1 reduce-scatter.10
  1207.4 105.4 all-reduce.12
where the time goes:
time: 1340 us; the launch traced here: 1330 us
  waiting for transfers between devices  531 us (40%)
  matrix products  475 us (35%)
  other arithmetic  137 us (10%)
  blocking collectives  125 us (9%)
  local copies, waits for them, and re-layouts  42.8 us (3%)
  between operations  17.3 us (1%)
    reduce_scatter x1, waiting for transfers between devices, body(): lax.psum_scatter(grad_wdown.astype(jnp.bfloat16), 'shard', scatter_dimens...  148 us
    reduce_scatter x1, waiting for transfers between devices, body(): lax.psum_scatter(grad_wup.astype(jnp.bfloat16), 'shard', scatter_dimensio...  144 us
    all_gather x1, waiting for transfers between devices, body(): lax.all_gather(w_down, 'shard', axis=0, tiled=True)  94.9 us
    dot_general x4, matrix products, matmul(): return jnp.dot(left, right, preferred_element_type=jnp.float32)  88.1 us
    psum x1, waiting for transfers between devices, body(): lax.psum(o_qkv.astype(jnp.bfloat16), 'rep').astype(jnp.float32)  85.5 us
    dot_general x4, matrix products, backward_group(): jnp.einsum('cqhd,ckhd->chqk', grad_part, value_part, preferred_element_ty...  70.2 us
    dot_general x4, matrix products, right_trans(): lax.dot_general(left, right, (((1,), (1,)), ((), ())), preferred_element_...  61 us
    dot_general x4, matrix products, left_trans(): lax.dot_general(left, right, (((0,), (0,)), ((), ())), preferred_element_...  55.5 us
  transfers between devices with their start and end apart: 9, of which 6 were waited for; matrix products, arithmetic and copies ran while one was open for 43% of the time, Pallas kernels for 0%

commit v1 on v0

--- a/solution.py
+++ b/solution.py
@@ -7,6 +7,27 @@
 HDIM = 64
 eps = 1e-06
 head_block = 4
+
+
+def joined_along(parts, dim):
+    parts = jnp.moveaxis(parts, 0, dim)
+    dims = parts.shape
+    return parts.reshape(*dims[:dim], dims[dim] * dims[dim + 1], *dims[dim + 2 :])
+
+
+def grow_blocks(value, axis):
+    length, position = (lax.axis_size(axis), lax.axis_index(axis))
+    pieces, bit = (value[None], 1)
+    while bit < length:
+        theirs = lax.ppermute(pieces, axis, [(i, i ^ bit) for i in range(length)])
+        low = position & bit == 0
+        pieces = jnp.concatenate([jnp.where(low, pieces, theirs), jnp.where(low, theirs, pieces)])
+        bit *= 2
+    return pieces
+
+
+def doubled_up(array, axis, dim):
+    return joined_along(grow_blocks(array, axis), dim)
 
 
 def layer_norm(values, gain, shift):
@@ -63,7 +84,7 @@
         lax.all_gather(ln2_shift, "shard", axis=0, tiled=True),
         lax.all_gather(w_up, "shard", axis=0, tiled=True),
         lax.all_gather(up_bias, "shard", axis=0, tiled=True),
-        lax.all_gather(w_down, "shard", axis=0, tiled=True),
+        doubled_up(w_down, "shard", 0),
         lax.all_gather(down_bias, "shard", axis=0, tiled=True),
     )
     (

time: 1340 us -> 1540 us (1.15)
  blocking collectives: 125 us -> 286 us
  waiting for transfers between devices: 531 us -> 562 us
    ppermute x0 -> x2, waiting for transfers between devices: none -> 291 us  [grow_blocks(): theirs = lax.ppermute(pieces, axis, [(i, i ^ bit) for i in range(length)])]
    all_gather x1, blocking collectives: 8.1 us -> 172 us  [body(): lax.all_gather(down_bias, 'shard', axis=0, tiled=True)]
    reduce_scatter x1, waiting for transfers between devices: 144 us -> 0.01 us  [body(): lax.psum_scatter(grad_wup.astype(jnp.bfloat16), 'shard', scatter_dimensio...]
    reduce_scatter x1, waiting for transfers between devices: 148 us -> 29.8 us  [body(): lax.psum_scatter(grad_wdown.astype(jnp.bfloat16), 'shard', scatter_dimens...]
  transfers between devices with their start and end apart: 9 -> 11, of which waited for: 6 -> 7; matrix products, arithmetic and copies ran while one was open for 43% -> 38% of each run, Pallas kernels for 0% -> 0%
where the time goes in v1:
time: 1540 us; the launch traced here: 1530 us
  waiting for transfers between devices  562 us (36%)
  matrix products  474 us (31%)
  blocking collectives  286 us (19%)
  other arithmetic  152 us (10%)
  local copies, waits for them, and re-layouts  41.8 us (3%)
  between operations  17.4 us (1%)
    ppermute x2, waiting for transfers between devices, grow_blocks(): theirs = lax.ppermute(pieces, axis, [(i, i ^ bit) for i in range(length)])  291 us
    all_gather x1, blocking collectives, body(): lax.all_gather(down_bias, 'shard', axis=0, tiled=True)  172 us
    all_gather x1, waiting for transfers between devices, body(): lax.all_gather(w_down, 'shard', axis=0, tiled=True)  95 us
    dot_general x4, matrix products, matmul(): return jnp.dot(left, right, preferred_element_type=jnp.float32)  87.5 us
    psum x1, waiting for transfers between devices, body(): lax.psum(o_qkv.astype(jnp.bfloat16), 'rep').astype(jnp.float32)  82.6 us
    dot_general x4, matrix products, backward_group(): jnp.einsum('cqhd,ckhd->chqk', grad_part, value_part, preferred_element_ty...  66.7 us
    dot_general x4, matrix products, right_trans(): lax.dot_general(left, right, (((1,), (1,)), ((), ())), preferred_element_...  61 us
    dot_general x4, matrix products, left_trans(): lax.dot_general(left, right, (((0,), (0,)), ((), ())), preferred_element_...  55.6 us
  transfers between devices with their start and end apart: 11, of which 7 were waited for; matrix products, arithmetic and copies ran while one was open for 38% of the time, Pallas kernels for 0%

profile of v1, /device:TPU:0, one launch (start us, length us, event | category | flops | bytes accessed | tf_op | source)
XLA Modules:
  0.0 1534.4 jit_solution(9716562958817226974)
XLA Ops:
  11.9 12.6 all-gather
  32.3 12.1 all-gather.2
  63.7 15.2 all-gather.5
  79.4 16.0 %all_gather.48 = bf16[4096]{0:T(1024)(128)(2,1)S(1)} all-gather(bf16[1024]{0:T(1024)(128)(2,1)S(1)} %copy-done.48), channel_id=1, replica_groups=mesh['rep'=8,'shard'=4] {'shard'}, dimensions={0}, use_global_device_ids=true | all-gather | bytes 10240 | tf_op jit(solution)/shard_map/all_gather | solution.py:86
  96.6 31.5 %all-gather.12.cloned.1.call-done = bf16[1024,3072]{1,0:T(8,128)(2,1)} async-done(((bf16[256,3072]{1,0:T(8,128)(2,1)}), bf16[1024,3072]{1,0:T(8,128)(2,1)}) %all-gather.12.cloned.1.call-update) | async-done | bytes 6291472 | tf_op jit(solution)/shard_map/all_gather | solution.py:79
  153.7 130.5 %while.26 = (s32[]{:T(128)}, bf16[4,1,1104,4,64]{2,4,3,1,0:T(8,128)(2,1)}, f32[4,1,4,1104]{3,2,1,0:T(4,128)}, bf16[4,1,1104,4,64]{2,4,3,1,0:T(8,128)(2,1)}, bf16...) while((s32[]{:T(128)}, bf16[4,1,1104,4,64]{2,4,3,1,0:T(8,128)(2,1)}, ...), condition=%wide.region_5.6_spmd, body=%wide.region_2.5_spmd.sunk | while | flops 1282190080 | bytes 62444876 | solution.py:149
  153.9 10.7 fusion.129
  174.8 11.9 fusion.131
  186.7 10.8 fusion.129
  207.7 11.5 fusion.131
  219.2 10.8 fusion.129
  240.2 11.5 fusion.131
  251.6 10.8 fusion.129
  272.6 11.5 fusion.131
  294.4 29.4 %all-gather.16.cloned.1.call-done = bf16[1024,4096]{1,0:T(8,128)(2,1)} async-done(((bf16[256,4096]{1,0:T(8,128)(2,1)}), bf16[1024,4096]{1,0:T(8,128)(2,1)}) %all-gather.16.cloned.1.call-update) | async-done | bytes 8388624 | tf_op jit(solution)/shard_map/all_gather | solution.py:85
  323.9 54.4 %multiply_convert_fusion.1 = (bf16[1104,4096]{1,0:T(8,128)(2,1)}, f32[1104,4096]{1,0:T(8,128)}, f32[1104,4096]{1,0:T(8,128)}) fusion(f32[4096]{0:T(1024)S(1)} %copy-done.40, bf16[1024,4096]{1,0:T(8,128)(2,1)} %all-gather.16.cloned.1.call-done, f32[1104,1024]{1,0:T(8,128)} %copy-done.10, f32[1024]{0:T(1024)S(1)} %bitcast.262, f32[1024]{0:T(1024)S(1)} %bitcast.254, ...), kind=kOutput, calls=%fused_computation.56 | convolution fusion | flops 9565126656 | bytes 58163840 | tf_op jit(solution)/shard_map/dot_general | solution.py:44
  378.2 95.0 %all-gather.18.cloned.1.call-done = bf16[4096,1024]{1,0:T(8,128)(2,1)} async-done(((bf16[1024,1024]{1,0:T(8,128)(2,1)}), bf16[4096,1024]{1,0:T(8,128)(2,1)}) %all-gather.18.cloned.1.call-update) | async-done | bytes 8388624 | tf_op jit(solution)/shard_map/all_gather | solution.py:172
  473.2 25.4 %fusion.92 = (bf16[4096]{0:T(1024)(128)(2,1)}, bf16[1104,4096]{1,0:T(8,128)(2,1)}) fusion(f32[1104,4096]{1,0:T(8,128)} %get-tuple-element.193, f32[1104,4096]{1,0:T(8,128)} %get-tuple-element.210, bf16[4096,1024]{1,0:T(8,128)(2,1)} %all-gather.18.cloned.1.call-done, bf16[1,1,1104,1024]{3,2,1,0:T(8,128)(2,1)S(1)} %copy-done.6, f32[]{:T(128)} %bitcast.22), kind=kOutput, calls=%fused_computation.143 | convolution fusion | flops 9332240384 | bytes 55877636 | tf_op jit(solution)/shard_map/dot_general | solution.py:54
  498.6 18.1 %multiply_reduce_fusion.1 = (bf16[1024]{0:T(1024)(128)(2,1)}, f32[1104]{0:T(1024)S(1)}, bf16[1024]{0:T(1024)(128)(2,1)}, f32[1104,1024]{1,0:T(8,128)S(1)}) fusion(f32[1104,1024]{1,0:T(8,128)} %copy-done.10, f32[1104]{0:T(1024)S(1)} %fusion.76, f32[1104]{0:T(1024)S(1)} %broadcast_multiply_fusion, f32[1024]{0:T(1024)S(1)} %bitcast.255, ...), kind=kOutput, calls=%fused_computation.103 | convolution fusion | flops 9270064128 | bytes 26497984 | tf_op jit(solution)/shard_map/dot_general | solution.py:54
  538.7 243.3 %while.27 = (s32[]{:T(128)}, bf16[4,1,1104,4,64]{2,4,3,1,0:T(8,128)(2,1)}, bf16[4,1,1104,4,64]{2,4,3,1,0:T(8,128)(2,1)}, bf16[4,1,1104,4,64]{2,4,3,1,0:T(8,128)(...) while((s32[]{:T(128)}, ...), condition=%wide.region_12.13_spmd, body=%wide.region_10.12_spmd.sunk | while | flops 3159731968 | bytes 201783552 | solution.py:224
  539.5 11.1 fusion.140
  550.6 16.8 %multiply_reduce_fusion.5 = (f32[4,1104]{1,0:T(4,128)S(1)}, f32[4,1104,1104]{1,2,0:T(8,128)}) fusion(f32[4,1104,1104]{1,2,0:T(8,128)} %fusion.140, bf16[4,1,1104,4,64]{2,4,3,1,0:T(8,128)(2,1)} %get-tuple-element.364, s32[]{:T(128)} %get-tuple-element.346, bf16[4,1,1104,4,64]{2,4,3,1,0:T(8,128)(2,1)S(1)} %copy-done.5), kind=kOutput, calls=%fused_computation.20.clone.1 | convolution fusion | flops 633779904 | bytes 41048320 | tf_op jit(solution)/shard_map/while/body/eval_jaxpr/cqhd,ckhd->chqk/dot_general | solution.py:204
  567.3 13.6 multiply_convert_fusion.3
  588.9 10.8 fusion.143
  600.4 11.0 fusion.140
  611.4 16.6 %multiply_reduce_fusion.5 = (f32[4,1104]{1,0:T(4,128)S(1)}, f32[4,1104,1104]{1,2,0:T(8,128)}) fusion(f32[4,1104,1104]{1,2,0:T(8,128)} %fusion.140, bf16[4,1,1104,4,64]{2,4,3,1,0:T(8,128)(2,1)} %get-tuple-element.364, s32[]{:T(128)} %get-tuple-element.346, bf16[4,1,1104,4,64]{2,4,3,1,0:T(8,128)(2,1)S(1)} %copy-done.5), kind=kOutput, calls=%fused_computation.20.clone.1 | convolution fusion | flops 633779904 | bytes 41048320 | tf_op jit(solution)/shard_map/while/body/eval_jaxpr/cqhd,ckhd->chqk/dot_general | solution.py:204
  628.1 13.5 multiply_convert_fusion.3
  649.6 10.8 fusion.143
  661.1 11.0 fusion.140
  672.2 16.6 %multiply_reduce_fusion.5 = (f32[4,1104]{1,0:T(4,128)S(1)}, f32[4,1104,1104]{1,2,0:T(8,128)}) fusion(f32[4,1104,1104]{1,2,0:T(8,128)} %fusion.140, bf16[4,1,1104,4,64]{2,4,3,1,0:T(8,128)(2,1)} %get-tuple-element.364, s32[]{:T(128)} %get-tuple-element.346, bf16[4,1,1104,4,64]{2,4,3,1,0:T(8,128)(2,1)S(1)} %copy-done.5), kind=kOutput, calls=%fused_computation.20.clone.1 | convolution fusion | flops 633779904 | bytes 41048320 | tf_op jit(solution)/shard_map/while/body/eval_jaxpr/cqhd,ckhd->chqk/dot_general | solution.py:204
  688.8 13.5 multiply_convert_fusion.3
  710.3 10.8 fusion.143
  721.8 11.0 fusion.140
  732.9 16.6 %multiply_reduce_fusion.5 = (f32[4,1104]{1,0:T(4,128)S(1)}, f32[4,1104,1104]{1,2,0:T(8,128)}) fusion(f32[4,1104,1104]{1,2,0:T(8,128)} %fusion.140, bf16[4,1,1104,4,64]{2,4,3,1,0:T(8,128)(2,1)} %get-tuple-element.364, s32[]{:T(128)} %get-tuple-element.346, bf16[4,1,1104,4,64]{2,4,3,1,0:T(8,128)(2,1)S(1)} %copy-done.5), kind=kOutput, calls=%fused_computation.20.clone.1 | convolution fusion | flops 633779904 | bytes 41048320 | tf_op jit(solution)/shard_map/while/body/eval_jaxpr/cqhd,ckhd->chqk/dot_general | solution.py:204
  749.5 13.5 multiply_convert_fusion.3
  771.0 10.8 fusion.143
  782.0 15.5 %convolution_convert_fusion.2 = bf16[1024,3072]{1,0:T(8,128)(2,1)} fusion(bf16[1,1,1104,1024]{3,2,1,0:T(8,128)(2,1)} %param.19, f32[1024]{0:T(1024)S(1)} %bitcast.261, f32[1024]{0:T(1024)S(1)} %bitcast.250, f32[1104]{0:T(1024)S(1)} %copy-done.25, f32[1104]{0:T(1024)S(1)} %copy-done.23, bf16[1104,1024]{0,1:T(8,128)(2,1)} %bitcast.242, ...), kind=kOutput, calls=%fused_computation.76 | convolution fusion | flops 6976045056 | bytes 15352448 | tf_op jit(solution)/shard_map/dot_general | solution.py:48
  798.3 18.5 %convolution_convert_fusion.1 = bf16[1024,4096]{1,0:T(8,128)(2,1)} fusion(bf16[1104,4096]{1,0:T(8,128)(2,1)} %get-tuple-element.214, f32[1104,1024]{1,0:T(8,128)} %copy-done.10, f32[1024]{0:T(1024)S(1)} %bitcast.263, f32[1024]{0:T(1024)S(1)} %bitcast.257, f32[1104]{0:T(1024)S(1)} %copy-done.37, f32[1104]{0:T(1024)S(1)} %copy-done.27), kind=kOutput, calls=%fused_computation.72 | convolution fusion | flops 9270870016 | bytes 21971584 | tf_op jit(solution)/shard_map/dot_general | solution.py:48
  818.4 17.4 %convolution_convert_fusion = bf16[4096,1024]{1,0:T(8,128)(2,1)} fusion(bf16[1104,4096]{1,0:T(8,128)(2,1)} %get-tuple-element.192, bf16[1,1,1104,1024]{3,2,1,0:T(8,128)(2,1)S(1)} %copy-done.7, f32[]{:T(128)} %bitcast.22), kind=kOutput, calls=%fused_computation.71 | convolution fusion | flops 9268609024 | bytes 19693572 | tf_op jit(solution)/shard_map/dot_general | solution.py:48
  836.0 114.2 %collective-permute-done = bf16[1,1024,1024]{2,1,0:T(8,128)(2,1)} collective-permute-done((bf16[1,1024,1024]{2,1,0:T(8,128)(2,1)}, bf16[1,1024,1024]{2,1,0:T(8,128)(2,1)}, u32[]{:S(2)}, u32[]{:S(2)}) %collective-permute-start) | collective-permute-done | bytes 2097184 | tf_op jit(solution)/shard_map/ppermute | solution.py:22
  959.0 172.2 %all-gather.6 = bf16[4,1,256]{2,1,0:T(2,128)(2,1)S(1)} all-gather(bf16[1,1,256]{2,1,0:T(2,128)(2,1)S(1)} %reshape.276), channel_id=1, replica_groups=mesh['rep'=8,'shard'=4] {'shard'}, dimensions={0}, use_global_device_ids=true | all-gather | bytes 2560 | tf_op jit(solution)/shard_map/all_gather | solution.py:88
  1131.7 177.0 %collective-permute-done.1 = bf16[2,1024,1024]{2,1,0:T(8,128)(2,1)} collective-permute-done((bf16[2,1024,1024]{2,1,0:T(8,128)(2,1)}, bf16[2,1024,1024]{2,1,0:T(8,128)(2,1)}, u32[]{:S(2)}, u32[]{:S(2)}) %collective-permute-start.1) | collective-permute-done | bytes 4194336 | tf_op jit(solution)/shard_map/ppermute | solution.py:22
  1326.9 12.6 fusion.83
  1344.4 19.4 %all-reduce.10 = (bf16[1024]{0:T(1024)(128)(2,1)S(1)}, bf16[1024]{0:T(1024)(128)(2,1)S(1)}, bf16[2048]{0:T(1024)(128)(2,1)S(1)}, bf16[1024]{0:T(1024)(128)(2,1)S...) all-reduce(bf16[1024]{0:T(1024)(128)(2,1)S(1)} %get-tuple-element.1, ...), channel_id=2, replica_groups=mesh['rep'=8,'shard'=4] {'shard'}, use_global_device_ids=true, to_apply=%region_16.17.clone | all-reduce | flops 12288 | bytes 49152
  1364.3 13.1 all-reduce.8
  1382.0 29.8 %reduce-scatter.11.cloned.1.call-done = bf16[1024,1024]{1,0:T(8,128)(2,1)} async-done(((bf16[4096,1024]{1,0:T(8,128)(2,1)}), bf16[1024,1024]{1,0:T(8,128)(2,1)}) %reduce-scatter.11.cloned.1.call-update) | async-done | bytes 2097168 | tf_op jit(solution)/shard_map/reduce_scatter | solution.py:267
  1418.5 16.6 %fusion.72 = bf16[1,1,1104,1024]{3,2,1,0:T(8,128)(2,1)} fusion(f32[1104,1024]{1,0:T(8,128)} %copy-done.10, bf16[1104,4096]{1,0:T(8,128)(2,1)} %get-tuple-element.192, bf16[4096,1024]{1,0:T(8,128)(2,1)} %bitcast.245, f32[1024]{0:T(1024)S(1)} %bitcast.264, f32[]{:T(128)} %bitcast.22), kind=kOutput, calls=%fused_computation.115 | convolution fusion | flops 9265545216 | bytes 24219652 | tf_op jit(solution)/shard_map/dot_general | solution.py:44
  1435.2 82.6 %all-reduce.13.cloned.1.call-done = (bf16[256,3072]{1,0:T(8,128)(2,1)}, bf16[256,1024]{1,0:T(8,128)(2,1)}, bf16[256,4096]{1,0:T(8,128)(2,1)}, bf16[1024,1024]{1,0:T(8,128)(2,1)}) async-done(((bf16[256,3072]{1,0:T(8,128)(2,1)}, bf16[256,1024]{1,0:T(8,128)(2,1)}, bf16[256,4096]{1,0:T(8,128)(2,1)}, bf16[1024,1024]{1,0:T(8,128)(2,1)}), (bf16[256,3072]{1,0:T(8,128)(2,1)}, bf16[256,1024]{1,0:T(8,128)(2,1)}, ...) | async-done | bytes 6291472 | tf_op jit(solution)/shard_map/psum | solution.py:278
  (269 shorter events, 220.0 us)
Async XLA Ops:
  7.2 121.0 %all-gather.12.cloned.1.call-start = ((), (), s32[]{:S(2)}) async-start(), calls=%async_computation.4 | async-start | bytes 7864320 | tf_op jit(solution)/shard_map/all_gather | solution.py:79
  7.9 276.3 %all-gather.14.cloned.1.call-start = ((), (), s32[]{:S(2)}) async-start(), calls=%async_computation.5 | async-start | bytes 2621440 | tf_op jit(solution)/shard_map/all_gather | solution.py:81
  8.7 15.8 %copy-start.53 = (bf16[256]{0:T(256)(128)(2,1)S(1)}, bf16[256]{0:T(256)(128)(2,1)}, u32[]{:S(2)}) copy-start(bf16[256]{0:T(256)(128)(2,1)} %param.22) | copy-start | bytes 1540
  8.7 23.6 %copy-start.51 = (bf16[512]{0:T(512)(128)(2,1)S(1)}, bf16[512]{0:T(512)(128)(2,1)}, u32[]{:S(2)}) copy-start(bf16[512]{0:T(512)(128)(2,1)} %param.24) | copy-start | bytes 3076
  8.7 35.7 %copy-start.54 = (bf16[256]{0:T(256)(128)(2,1)S(1)}, bf16[256]{0:T(256)(128)(2,1)}, u32[]{:S(2)}) copy-start(bf16[256]{0:T(256)(128)(2,1)} %param.26) | copy-start | bytes 1540
  8.7 46.2 %copy-start.55 = (bf16[256]{0:T(256)(128)(2,1)S(1)}, bf16[256]{0:T(256)(128)(2,1)}, u32[]{:S(2)}) copy-start(bf16[256]{0:T(256)(128)(2,1)} %param.27) | copy-start | bytes 1540
  8.7 54.9 %copy-start.56 = (bf16[256]{0:T(256)(128)(2,1)S(1)}, bf16[256]{0:T(256)(128)(2,1)}, u32[]{:S(2)}) copy-start(bf16[256]{0:T(256)(128)(2,1)} %param.28) | copy-start | bytes 1540
  8.7 70.7 %copy-start.48 = (bf16[1024]{0:T(1024)(128)(2,1)S(1)}, bf16[1024]{0:T(1024)(128)(2,1)}, u32[]{:S(2)}) copy-start(bf16[1024]{0:T(1024)(128)(2,1)} %param.30) | copy-start | bytes 6148
  8.7 315.1 %all-gather.16.cloned.1.call-start = ((), (), s32[]{:S(2)}) async-start(), calls=%async_computation.6 | async-start | bytes 10485760 | tf_op jit(solution)/shard_map/all_gather | solution.py:85
  9.5 463.7 %all-gather.18.cloned.1.call-start = ((), (), s32[]{:S(2)}) async-start(), calls=%async_computation.7 | async-start | bytes 10485760 | tf_op jit(solution)/shard_map/all_gather | solution.py:172
  10.1 1371.9 %reduce-scatter.7.cloned.1.call-start = ((), (), s32[]{:S(2)}) async-start(), calls=%async_computation.9 | async-start | bytes 2621440 | tf_op jit(solution)/shard_map/reduce_scatter | solution.py:249
  10.5 127.3 %copy-start.22 = (f32[1104]{0:T(1024)}, f32[1104]{0:T(1024)S(1)}, u32[]{:S(2)}) copy-start(f32[1104]{0:T(1024)S(1)} %broadcast_multiply_fusion.1) | copy-start | bytes 13252
  11.9 126.0 %copy-start.24 = (f32[1104]{0:T(1024)}, f32[1104]{0:T(1024)S(1)}, u32[]{:S(2)}) copy-start(f32[1104]{0:T(1024)S(1)} %fusion.75) | copy-start | bytes 13252
  24.5 113.4 %copy-start.34 = (f32[4,1,256]{2,1,0:T(1,128)}, f32[4,1,256]{2,1,0:T(1,128)S(1)}, u32[]{:S(2)}) copy-start(f32[4,1,256]{2,1,0:T(1,128)S(1)} %convert_element_type.229) | copy-start | bytes 12292
  32.3 105.6 %copy-start.43 = (f32[4,1,256]{2,1,0:T(1,128)}, f32[4,1,256]{2,1,0:T(1,128)S(1)}, u32[]{:S(2)}) copy-start(f32[4,1,256]{2,1,0:T(1,128)S(1)} %convert_element_type.230) | copy-start | bytes 12292
  153.7 130.5 %copy-start.47 = (f32[4,1,256]{2,1,0:T(1,128)S(1)}, f32[4,1,256]{2,1,0:T(1,128)}, u32[]{:S(2)}) copy-start(f32[4,1,256]{2,1,0:T(1,128)} %convert_element_type.232) | copy-start | bytes 12292
  284.2 6.9 copy-start
  291.1 32.7 %copy-start.38 = (f32[4,1,256]{2,1,0:T(1,128)S(1)}, f32[4,1,256]{2,1,0:T(1,128)}, u32[]{:S(2)}) copy-start(f32[4,1,256]{2,1,0:T(1,128)} %convert_element_type.233) | copy-start | bytes 12292
  291.2 32.7 %copy-start.40 = (f32[4096]{0:T(1024)S(1)}, f32[4096]{0:T(1024)}, u32[]{:S(2)}) copy-start(f32[4096]{0:T(1024)} %convert_element_type.198) | copy-start | bytes 49156
  291.2 32.7 %copy-start.45 = (f32[4,1,256]{2,1,0:T(1,128)S(1)}, f32[4,1,256]{2,1,0:T(1,128)}, u32[]{:S(2)}) copy-start(f32[4,1,256]{2,1,0:T(1,128)} %convert_element_type.234) | copy-start | bytes 12292
  291.2 225.5 %copy-start.26 = (f32[1104]{0:T(1024)}, f32[1104]{0:T(1024)S(1)}, u32[]{:S(2)}) copy-start(f32[1104]{0:T(1024)S(1)} %broadcast_multiply_fusion) | copy-start | bytes 13252
  294.4 222.3 %copy-start.36 = (f32[1104]{0:T(1024)}, f32[1104]{0:T(1024)S(1)}, u32[]{:S(2)}) copy-start(f32[1104]{0:T(1024)S(1)} %fusion.76) | copy-start | bytes 13252
  323.8 149.3 %copy-start.6 = (bf16[1,1,1104,1024]{3,2,1,0:T(8,128)(2,1)S(1)}, bf16[1,1,1104,1024]{3,2,1,0:T(8,128)(2,1)}, u32[]{:S(2)}) copy-start(bf16[1,1,1104,1024]{3,2,1,0:T(8,128)(2,1)} %param.33) | copy-start | bytes 6782980
  498.5 18.1 %copy-start.31 = (f32[1104]{0:T(1024)S(1)}, f32[1104]{0:T(1024)}, u32[]{:S(2)}) copy-start(f32[1104]{0:T(1024)} %copy-done.30) | copy-start | bytes 13252
  498.5 18.2 %copy-start.11 = (f32[1104,1024]{1,0:T(8,128)S(1)}, f32[1104,1024]{1,0:T(8,128)}, u32[]{:S(2)}) copy-start(f32[1104,1024]{1,0:T(8,128)} %copy-done.10) | copy-start | bytes 13565956
  526.0 856.0 %reduce-scatter.5.cloned.1.call-start = ((), (), s32[]{:S(2)}) async-start(), calls=%async_computation.8 | async-start | bytes 7864320 | tf_op jit(solution)/shard_map/reduce_scatter | solution.py:243
  533.5 5.2 copy-start.1
  538.7 243.3 %copy-start.23 = (f32[1104]{0:T(1024)S(1)}, f32[1104]{0:T(1024)}, u32[]{:S(2)}) copy-start(f32[1104]{0:T(1024)} %copy-done.22) | copy-start | bytes 13252
  538.7 243.3 %copy-start.25 = (f32[1104]{0:T(1024)S(1)}, f32[1104]{0:T(1024)}, u32[]{:S(2)}) copy-start(f32[1104]{0:T(1024)} %copy-done.24) | copy-start | bytes 13252
  538.7 243.3 %copy-start.35 = (f32[4,1,256]{2,1,0:T(1,128)S(1)}, f32[4,1,256]{2,1,0:T(1,128)}, u32[]{:S(2)}) copy-start(f32[4,1,256]{2,1,0:T(1,128)} %copy-done.34) | copy-start | bytes 12292
  538.7 243.3 %copy-start.44 = (f32[4,1,256]{2,1,0:T(1,128)S(1)}, f32[4,1,256]{2,1,0:T(1,128)}, u32[]{:S(2)}) copy-start(f32[4,1,256]{2,1,0:T(1,128)} %copy-done.43) | copy-start | bytes 12292
  539.5 11.1 copy-start.5
  567.3 13.6 copy-start.15
  600.4 11.0 copy-start.5
  628.1 13.5 copy-start.15
  661.1 11.0 copy-start.5
  688.8 13.5 copy-start.15
  721.8 11.0 copy-start.5
  749.5 13.5 copy-start.15
  797.6 584.4 %reduce-scatter.9.cloned.1.call-start = ((), (), s32[]{:S(2)}) async-start(), calls=%async_computation.10 | async-start | bytes 10485760 | tf_op jit(solution)/shard_map/reduce_scatter | solution.py:261
  816.8 595.0 %reduce-scatter.11.cloned.1.call-start = ((), (), s32[]{:S(2)}) async-start(), calls=%async_computation.11 | async-start | bytes 10485760 | tf_op jit(solution)/shard_map/reduce_scatter | solution.py:267
  835.8 682.0 %all-reduce.13.cloned.1.call-start = ((), (), s32[]{:S(2)}) async-start(), calls=%async_computation.12 | async-start | bytes 12582912 | tf_op jit(solution)/shard_map/psum | solution.py:278
  835.9 114.3 %collective-permute-start = (bf16[1,1024,1024]{2,1,0:T(8,128)(2,1)}, bf16[1,1024,1024]{2,1,0:T(8,128)(2,1)}, u32[]{:S(2)}, u32[]{:S(2)}) collective-permute-start(bf16[1,1024,1024]{2,1,0:T(8,128)(2,1)} %bitcast.246), channel_id=1, source_target_pairs={{0,1},{1,0},{2,3},{3,2},{4,5},{5,4},{6,7},{7,6},{8,9},{9,8},{10,11... | collective-permute-start | bytes 6291464 | tf_op jit(solution)/shard_map/ppermute | solution.py:22
  952.7 6.3 copy-start.57
  956.4 352.4 %collective-permute-start.1 = (bf16[2,1024,1024]{2,1,0:T(8,128)(2,1)}, bf16[2,1024,1024]{2,1,0:T(8,128)(2,1)}, u32[]{:S(2)}, u32[]{:S(2)}) collective-permute-start(bf16[2,1024,1024]{2,1,0:T(8,128)(2,1)} %pad_maximum_fusion.2), channel_id=1, source_target_pairs={{0,2},{1,3},{2,0},{3,1},{4,6},{5,7},{6,4},{7,5},{8,10},{9,11},{10,... | collective-permute-start | bytes 12582920 | tf_op jit(solution)/shard_map/ppermute | solution.py:22
  1326.9 12.7 copy-start.29
  1339.6 4.7 copy-start.41
  1344.3 67.5 %copy-start.33 = (f32[1104]{0:T(1024)S(1)}, f32[1104]{0:T(1024)}, u32[]{:S(2)}) copy-start(f32[1104]{0:T(1024)} %copy-done.32) | copy-start | bytes 13252
  (37 other events, 97.3 us)
Sparse Core Ops, SparseCore 0:
  9.6 118.5 all-gather.11
  129.8 44.0 all-gather.13
  175.5 148.3 all-gather.15
  325.3 147.8 all-gather.17
  526.1 42.0 reduce-scatter.6
  797.7 152.0 reduce-scatter.4
  952.3 286.6 reduce-scatter.8
  1241.4 170.2 reduce-scatter.10
  1415.8 101.9 all-reduce.12
